TPU v7x, 32 devices: a whole 2x2x4 slice. The times are simulated.
32 devices in a mesh: space: 8 (over y, x, core), sample: 4 (over z).
Axes of the slice: x: 2, y: 2, z: 4, core: 2. Of those that a mesh axis runs over, the one named last changes fastest.
Arguments:
- fields: bfloat16 [4, 64, 20, 8192], P('sample', 'space'), may hold values from -6 to 6
- cotangent: bfloat16 [4, 64, 20, 8192], P('sample', 'space'), may hold values from -6 to 6
- spectral_weight: bfloat16 [2, 20, 20, 4608], P(None, None, None, 'space'), may hold values from -6 to 6
- point_weight: bfloat16 [20, 20], replicated, may hold values from -1.25 to 1.25
- point_bias: float32 [20], replicated, may hold values from -1 to 1
Outputs:
- activated: bfloat16 [4, 64, 20, 8192], P('sample', 'space')
- grad_input: bfloat16 [4, 64, 20, 8192], P('sample', 'space')
- grad_spectral: float32 [2, 20, 20, 4608], P(None, None, None, ('space', 'sample'))
All inputs are finite; a program needn't handle non-finite values.
Results may differ from a plain program's by a relative error of at most 0.001.
Values sent between devices are 32-bit elements; how exact they have to be, the bound alone decides.
A program may use at most 128 MiB of HBM per device.

v0:
```python
import functools
import math

import jax
import jax.numpy as jnp
import numpy as np
from jax import lax
from jax.experimental import pallas as pl
from jax.experimental.pallas import tpu as pltpu
from jax.sharding import PartitionSpec as P

NX, NY, NZ, NT = 64, 64, 32, 4
MX, MY, MZ, MT = 12, 12, 8, 4
VOLUME = NX * NY * NZ * NT
PLANE = NZ * NT
XY = MX * MY
BF16, F32 = jnp.bfloat16, jnp.float32
VMEM_LIMIT = 60 * 1024 * 1024


def signed(modes):
    index = np.arange(modes)
    return np.where(index < modes // 2, index, index - modes)


def split_np(table):
    high = table.astype(np.float32).astype(BF16)
    low = (table - high.astype(np.float64)).astype(np.float32).astype(BF16)
    return high, low


def tables(rows, space):
    y, x = np.arange(NY)[:, None], np.arange(rows)[None, :]
    fy, fx = signed(MY)[:, None], signed(MX)[None, :]
    phi = 2 * np.pi * (
        fy.reshape(MY, 1, 1, 1) * y.reshape(1, 1, NY, 1) / NY
        + fx.reshape(1, MX, 1, 1) * x.reshape(1, 1, 1, rows) / NX
    ).reshape(XY, NY * rows)
    plane = np.concatenate([np.cos(phi), np.sin(phi)], 0)
    hi, lo = split_np(plane)
    forward = np.concatenate([hi, lo], 0)
    inverse = np.concatenate([hi.T, lo.T], 0)
    fz, ft = signed(MZ), signed(MT)
    z, t = np.arange(NZ), np.arange(NT)
    psi = 2 * np.pi * (
        fz.reshape(MZ, 1, 1, 1) * z.reshape(1, 1, NZ, 1) / NZ
        + ft.reshape(1, MT, 1, 1) * t.reshape(1, 1, 1, NT) / NT
    ).reshape(space, MZ * MT // space, PLANE)
    cos, sin = np.cos(psi), np.sin(psi)
    depth = np.stack(
        [np.concatenate([cos, -sin], -1), np.concatenate([-sin, -cos], -1)], 1
    ).reshape(MZ * 2 * MT, 2 * PLANE)
    dhi, dlo = split_np(depth)
    depth_forward = np.concatenate([dhi, dlo], 0)
    depth_inverse = np.concatenate([dhi, dhi, dlo], 0)
    return forward, inverse, depth_forward, depth_inverse


def split(value):
    high = value.astype(BF16)
    return high, (value - high.astype(F32)).astype(BF16)


def dot(a, b):
    return lax.dot_general(a, b, (((1,), (0,)), ((), ())), preferred_element_type=F32)


def forward_transform(src, fwd, depth, zhi, zlo, out, exact):
    channels = src.shape[0]
    half = fwd.shape[0] // 2

    def pair(g, carry):
        block = jnp.concatenate([src[2 * g], src[2 * g + 1]], -1)
        if exact:
            res = dot(fwd[...], block.astype(BF16))
            res = res[:half] + res[half:]
        else:
            high, low = split(block)
            res = dot(fwd[...], high)
            res = res[:half] + res[half:] + dot(fwd[:half], low)
        for k in range(2):
            part = res[:, k * PLANE : (k + 1) * PLANE]
            high, low = split(jnp.concatenate([part[:XY], part[XY:]], -1))
            zhi[2 * g + k] = high
            zlo[2 * g + k] = low
        return carry

    lax.fori_loop(0, channels // 2, pair, 0, unroll=2)
    rows = out.shape[0]
    contract = (((1,), (1,)), ((), ()))
    high = zhi[...].reshape(channels * XY, 2 * PLANE)
    low = zlo[...].reshape(channels * XY, 2 * PLANE)
    first = lax.dot_general(depth[...], high, contract, preferred_element_type=F32)
    second = lax.dot_general(depth[:rows], low, contract, preferred_element_type=F32)
    out[...] = first[:rows] + first[rows:] + second


def inverse_transform(modes, depth, inv, ghi, glo, dst):
    outputs = dst.shape[0]
    cells = inv.shape[0] // 2
    high, low = split(modes[...])
    stacked = jnp.concatenate([high, low, high], 0)
    lines = lax.dot_general(
        stacked, depth[...], (((0,), (0,)), ((), ())), preferred_element_type=F32
    )
    high, low = split(lines.reshape(outputs, XY, 2 * PLANE))
    ghi[:, :XY] = high[:, :, :PLANE]
    ghi[:, XY:] = high[:, :, PLANE:]
    glo[:, :XY] = low[:, :, :PLANE]
    glo[:, XY:] = low[:, :, PLANE:]

    def pair(g, carry):
        high = jnp.concatenate([ghi[2 * g], ghi[2 * g + 1]], -1)
        low = jnp.concatenate([glo[2 * g], glo[2 * g + 1]], -1)
        res = dot(inv[...], high)
        res = res[:cells] + res[cells:] + dot(inv[:cells], low)
        dst[2 * g] = res[:, :PLANE]
        dst[2 * g + 1] = res[:, PLANE:]
        return carry

    lax.fori_loop(0, outputs // 2, pair, 0, unroll=2)


def first_kernel(fields, fwd, depth, out, src, zhi, zlo):
    rows = fields.shape[1]

    def line(i, carry):
        at = pl.multiple_of(i * PLANE, PLANE)
        to = pl.multiple_of(i * rows, rows)
        src[:, pl.ds(to, rows), :] = fields[:, :, pl.ds(at, PLANE)].astype(F32)
        return carry

    lax.fori_loop(0, NY, line, 0, unroll=4)
    forward_transform(src, fwd, depth, zhi, zlo, out, True)


def middle_kernel(
    modes, fields, cot, point, point_t, bias_row, copies, copies_t, same, fwd, inv, depth, depth_inv,
    activated, local, out, work, ghi, glo, zhi, zlo, mix, mix_back, bias,
):
    channels, rows, _ = fields.shape
    inverse_transform(modes, depth_inv, inv, ghi, glo, work)
    flat = channels * rows

    def spread(matrix):
        half = dot(copies[...], matrix).astype(BF16)
        return dot(half, copies_t[...]).astype(BF16) * same[...]

    mix_back[...] = spread(point[...])
    mix[...] = spread(point_t[...])
    column = jnp.sum(copies[...].astype(F32) * bias_row[...], -1, keepdims=True)
    bias[...] = jnp.broadcast_to(column, (flat, PLANE))

    def line(i, carry):
        at = pl.multiple_of(i * 2 * PLANE, 2 * PLANE)
        block = fields[:, :, pl.ds(at, 2 * PLANE)].astype(F32)
        near = dot(mix[...], block.reshape(flat, 2 * PLANE).astype(BF16))
        ups = []
        for k in range(2):
            here = pl.multiple_of(at + k * PLANE, PLANE)
            to = pl.multiple_of((2 * i + k) * rows, rows)
            far = work[:, pl.ds(to, rows), :].reshape(flat, PLANE)
            pre = far + near[:, k * PLANE : (k + 1) * PLANE] + bias[...]
            phi = 0.5 * (1.0 + lax.erf(pre * (1.0 / math.sqrt(2.0))))
            slope = phi + pre * jnp.exp(-0.5 * pre * pre) * (1.0 / math.sqrt(2.0 * math.pi))
            act = (pre * phi).reshape(channels, rows, PLANE)
            activated[:, :, pl.ds(here, PLANE)] = act.astype(BF16)
            c = cot[:, :, pl.ds(here, PLANE)].astype(F32).reshape(flat, PLANE)
            up = c * slope
            work[:, pl.ds(to, rows), :] = up.reshape(channels, rows, PLANE)
            ups.append(up)
        high, low = split(jnp.concatenate(ups, -1))
        back = dot(mix_back[...], high) + dot(mix_back[...], low)
        local[:, :, pl.ds(at, 2 * PLANE)] = back.reshape(channels, rows, 2 * PLANE)
        return carry

    lax.fori_loop(0, NY // 2, line, 0, unroll=2)
    forward_transform(work, fwd, depth, zhi, zlo, out, False)


def last_kernel(modes, local, spec_all, up_all, inv, depth_inv, out, grad, work, ghi, glo):
    rows = local.shape[1]
    samples, _, channels, count = spec_all.shape
    inverse_transform(modes, depth_inv, inv, ghi, glo, work)

    def line(i, carry):
        at = pl.multiple_of(i * PLANE, PLANE)
        to = pl.multiple_of(i * rows, rows)
        value = work[:, pl.ds(to, rows), :] + local[:, :, pl.ds(at, PLANE)]
        out[:, :, pl.ds(at, PLANE)] = value.astype(BF16)
        return carry

    lax.fori_loop(0, NY, line, 0, unroll=4)

    def term(c, carry):
        real = jnp.zeros((channels, count), F32)
        imag = jnp.zeros((channels, count), F32)
        for s in range(samples):
            a_r, a_i = spec_all[s, 0, pl.ds(c, 1), :], spec_all[s, 1, pl.ds(c, 1), :]
            b_r, b_i = up_all[s, 0], up_all[s, 1]
            real = real + (a_r * b_r + a_i * b_i)
            imag = imag + (a_r * b_i - a_i * b_r)
        grad[c, :, 0, :] = real
        grad[c, :, 1, :] = imag
        return carry

    lax.fori_loop(0, channels, term, 0)


def call(body, outs, scratch):
    return pl.pallas_call(
        body,
        out_shape=outs,
        scratch_shapes=scratch,
        compiler_params=pltpu.CompilerParams(vmem_limit_bytes=VMEM_LIMIT),
    )


def swap(value):
    half = value.shape[0] // 2
    return jnp.concatenate([value[half:], value[:half]], 0)


def exchange_kernel(n, ns, backward, scale_in, scale_out, *refs):
    if backward:
        (partial, weight, cos, sin, spec_in, modes, spec_all, up_all,
         recv, stage, lined, out_lined, mixed, gat, pre, joined, gat_near, s_got, u_got, spec,
         send_a, recv_a, send_b, recv_b, send_c, recv_c, send_d, recv_d, send_s, recv_s, send_u, recv_u) = refs
    else:
        (partial, weight, cos, sin, modes, spec,
         recv, stage, lined, out_lined, mixed, gat, pre, joined, gat_near, send_a, recv_a, send_b, recv_b, send_c, recv_c, send_d, recv_d) = refs
    _, rows, lanes = partial.shape
    channels, width = stage.shape[0], stage.shape[2]
    owned = rows // 2
    per = ns // owned
    count = width // per
    me = lax.axis_index("space")
    mine = lax.axis_index("sample")

    barrier = pltpu.get_barrier_semaphore()
    for k in range(1, n):
        pl.semaphore_signal(
            barrier, inc=1, device_id={"space": lax.rem(me + k, n)},
            device_id_type=pl.DeviceIdType.MESH,
        )
    if backward:
        for k in range(1, ns):
            pl.semaphore_signal(
                barrier, inc=1, device_id={"sample": lax.rem(mine + k, ns)},
                device_id_type=pl.DeviceIdType.MESH,
            )
    pl.semaphore_wait(barrier, n - 1 + (ns - 1 if backward else 0))

    def start(src, dst, send, got, k, axis, target):
        copy = pltpu.make_async_remote_copy(
            src_ref=src, dst_ref=dst.at[k], send_sem=send.at[k], recv_sem=got.at[k],
            device_id={axis: target}, device_id_type=pl.DeviceIdType.MESH,
        )
        copy.start()
        return copy

    sibling = me + 1 - 2 * lax.rem(me, 2)
    near = {}
    for k in range(0, n, 2):
        target = lax.rem(sibling + k, n)
        near[k] = start(partial.at[target], pre, send_d, recv_d, k, "space", sibling)
    side = []
    if backward:
        for k in range(1, ns):
            target = lax.rem(mine + k, ns)
            side.append(start(spec_in.at[target], s_got, send_s, recv_s, k, "sample", target))

    row = lax.broadcasted_iota(jnp.int32, (rows, lanes), 0)
    top = row < rows // 2

    def turn(value, source):
        c, s = cos[pl.ds(source, 1), :], sin[pl.ds(source, 1), :]
        turned = swap(value) * s
        return value * c + jnp.where(top, turned, -turned)

    first = {}
    for k in list(range(2, n, 2)) + [0]:
        near[k].wait()
        target = lax.rem(me + k, n)
        joined[k] = turn(partial[target], me) + turn(pre[k], sibling)
        if k:
            first[k] = start(joined.at[k], recv, send_a, recv_a, k, "space", target)
    total = joined[0]
    for k in range(2, n, 2):
        first[k].wait()
        total = total + recv[k]
    total = total * scale_in
    for c in range(channels):
        stage[c] = total[:, c * width : (c + 1) * width]
    for j in range(rows):
        r, q = j // owned, j % owned
        block = stage[:, j, :]
        lined[r, :, q * width : (q + 1) * width] = block
        for p in range(per):
            spec[q * per + p, r] = block[:, p * count : (p + 1) * count]
    if backward:
        for k in range(1, ns):
            target = lax.rem(mine + k, ns)
            side.append(start(spec.at[target], u_got, send_u, recv_u, k, "sample", target))

    if backward:

        def reduce(c, carry):
            w_r, w_i = weight[0, c], weight[1, c]
            u_r, u_i = lined[0], lined[1]
            out_lined[0, pl.ds(c, 1), :] = jnp.sum(w_r * u_r + w_i * u_i, 0, keepdims=True)
            out_lined[1, pl.ds(c, 1), :] = jnp.sum(w_r * u_i - w_i * u_r, 0, keepdims=True)
            return carry

        lax.fori_loop(0, channels, reduce, 0)
    else:

        def add(c, carry):
            w_r, w_i = weight[0, c], weight[1, c]
            s_r, s_i = lined[0, pl.ds(c, 1), :], lined[1, pl.ds(c, 1), :]
            return carry[0] + (w_r * s_r - w_i * s_i), carry[1] + (w_r * s_i + w_i * s_r)

        zero = jnp.zeros((channels, owned * width), F32)
        real, imag = lax.fori_loop(0, channels, add, (zero, zero))
        out_lined[0] = real
        out_lined[1] = imag
    for j in range(rows):
        r, q = j // owned, j % owned
        stage[:, j, :] = out_lined[r, :, q * width : (q + 1) * width]
    for c in range(channels):
        mixed[:, c * width : (c + 1) * width] = stage[c]

    second, relay = {}, {}
    for k in range(2, n, 2):
        second[k] = start(mixed, gat, send_b, recv_b, k, "space", lax.rem(me + k, n))
    relay[0] = start(mixed, gat_near, send_c, recv_c, 0, "space", sibling)
    c, s = cos[pl.ds(me, 1), :] * scale_out, sin[pl.ds(me, 1), :] * scale_out
    signed_s = jnp.where(top, -s, s)

    def place(value, source):
        modes[source] = value * c + swap(value) * signed_s

    place(mixed[...], me)
    for k in range(2, n, 2):
        second[k].wait()
        relay[k] = start(gat.at[k], gat_near, send_c, recv_c, k, "space", sibling)
        place(gat[k], lax.rem(me + n - k, n))
    for k in range(0, n, 2):
        relay[k].wait()
        place(gat_near[k], lax.rem(sibling + n - k, n))
    if backward:
        for copy in side:
            copy.wait()
        spec_all[0] = spec_in[mine]
        up_all[0] = spec[mine]
        for k in range(1, ns):
            spec_all[k] = s_got[k]
            up_all[k] = u_got[k]


def exchange(partial, weight, cos, sin, spec_in, n, ns, scale_in, scale_out):
    backward = spec_in is not None
    _, channels, _, modes = weight.shape
    _, rows, lanes = partial.shape
    many = jax.ShapeDtypeStruct((n, rows, lanes), F32)
    kept = (ns, 2, channels, modes // ns)
    outs = [many] if backward else [many, jax.ShapeDtypeStruct(kept, F32)]
    slot = pltpu.VMEM((n, rows, lanes), F32)
    line = pltpu.VMEM((2, channels, modes), F32)
    stage = pltpu.VMEM((channels, rows, lanes // channels), F32)
    scratch = [slot, stage, line, line, pltpu.VMEM((rows, lanes), F32), slot, slot, slot, slot]
    sems = [pltpu.SemaphoreType.DMA((n,))] * 8
    args = [partial, weight, cos, sin]
    if backward:
        outs += [jax.ShapeDtypeStruct(kept, F32)] * 2
        scratch += [pltpu.VMEM(kept, F32)] * 3
        sems += [pltpu.SemaphoreType.DMA((ns,))] * 4
        args.append(spec_in)
    vmem = pl.BlockSpec(memory_space=pltpu.VMEM)
    return pl.pallas_call(
        functools.partial(exchange_kernel, n, ns, backward, scale_in, scale_out),
        out_shape=outs,
        in_specs=[vmem] * len(args),
        out_specs=[vmem] * len(outs),
        scratch_shapes=scratch + sems,
        compiler_params=pltpu.CompilerParams(
            vmem_limit_bytes=VMEM_LIMIT, collective_id=int(backward), has_side_effects=True
        ),
    )(*args)


def shards(fields, cotangent, spectral_weight, point_weight, point_bias):
    _, rows, channels, columns = fields.shape
    space = lax.axis_size("space")
    samples = lax.axis_size("sample")
    fwd, inv, depth, depth_inv = [jnp.asarray(t) for t in tables(rows, space)]
    owned = MT * MZ // space
    own_rows = 2 * owned
    all_rows = 2 * MT * MZ
    lanes = channels * XY
    cells = NY * rows
    field = jnp.transpose(fields[0], (1, 0, 2))
    cot = jnp.transpose(cotangent[0], (1, 0, 2))
    flat = channels * rows
    copies = np.repeat(np.eye(channels), rows, 0).astype(BF16)
    same = np.tile(np.eye(rows), (channels, channels)).astype(BF16)
    flat_buf = pltpu.VMEM((flat, flat), BF16)

    freq = np.tile(signed(MX), MY * channels)
    angle = 2 * np.pi * (freq[None, :] * np.arange(space)[:, None] * rows % NX) / NX
    turn_cos = np.cos(angle).astype(np.float32)
    turn_sin = np.sin(angle).astype(np.float32)

    z_buf = pltpu.VMEM((channels, XY, 2 * PLANE), BF16)
    g_buf = pltpu.VMEM((channels, 2 * XY, PLANE), BF16)
    w_buf = pltpu.VMEM((channels, cells, PLANE), F32)
    part = jax.ShapeDtypeStruct((all_rows, lanes), F32)
    grid_bf = jax.ShapeDtypeStruct((channels, rows, columns), BF16)
    grid_f = jax.ShapeDtypeStruct((channels, rows, columns), F32)

    weights = spectral_weight.astype(F32)

    partial = call(first_kernel, part, [w_buf, z_buf, z_buf])(field, fwd, depth)
    split_part = lambda value: value.reshape(space, own_rows, lanes)
    modes, spec_in = exchange(
        split_part(partial), weights, turn_cos, turn_sin, None,
        space, samples, 1.0, 1.0 / VOLUME,
    )
    activated, local, partial_up = call(
        middle_kernel, (grid_bf, grid_f, part), [w_buf, g_buf, g_buf, z_buf, z_buf, flat_buf, flat_buf, pltpu.VMEM((flat, PLANE), F32)]
    )(
        modes.reshape(all_rows, lanes), field, cot, point_weight, point_weight.T,
        point_bias[None], copies, copies.T, same, fwd, inv, depth, depth_inv,
    )
    modes_back, spec_all, up_all = exchange(
        split_part(partial_up), weights, turn_cos, turn_sin, spec_in,
        space, samples, 1.0 / VOLUME, 1.0,
    )
    count = owned * XY // samples
    grad_shape = jax.ShapeDtypeStruct((channels, channels, 2, count), F32)
    grad_input, grad = call(last_kernel, (grid_bf, grad_shape), [w_buf, g_buf, g_buf])(
        modes_back.reshape(all_rows, lanes), local, spec_all, up_all, inv, depth_inv
    )
    grad_spectral = jnp.transpose(grad, (2, 0, 1, 3))
    back_to = lambda value: jnp.transpose(value, (1, 0, 2))[None]
    return back_to(activated), back_to(grad_input), grad_spectral


def solution(mesh):
    return jax.shard_map(
        shards,
        mesh=mesh,
        in_specs=(
            P("sample", "space", None, None),
            P("sample", "space", None, None),
            P(None, None, None, "space"),
            P(),
            P(),
        ),
        out_specs=(
            P("sample", "space", None, None),
            P("sample", "space", None, None),
            P(None, None, None, ("space", "sample")),
        ),
        check_vma=False,
    )
```

profile of v0, /device:TPU:0, one launch (start us, length us, event | category | flops | bytes accessed | tf_op | source)
XLA Modules:
  0.0 94.3 jit_solution(11038708942086124685)
XLA Ops:
  0.6 0.0 copy-start
  0.6 1.5 %copy.18 = bf16[20,20]{0,1:T(8,128)(2,1)} copy(bf16[20,20]{1,0:T(8,128)(2,1)} %point.1) | data formatting | bytes 1600 | tf_op args[3]
  2.1 7.0 %shard_map.157 = f32[64,2880]{1,0:T(8,128)} custom-call(bf16[20,8,8192]{2,1,0:T(8,128)(2,1)} %bitcast.19, bf16[576,512]{1,0:T(8,128)(2,1)} %constant.18.clone.fwd, bf16[128,256]{1,0:T(8,128)(2,1)} %constant.20.clone.depth), custom_call_target="tpu_custom_call" | custom-call | tf_op jit(solution)/shard_map/pallas_call | solution.py:423
  9.1 0.0 copy-done
  9.1 1.6 %copy_convert_fusion.refs_1_ = f32[2,20,20,576]{3,2,1,0:T(8,128)} fusion(bf16[2,20,20,576]{3,0,2,1:T(2,128)(2,1)S(1)} %copy-done), kind=kLoop, calls=%fused_computation | loop fusion | flops 460800 | bytes 2764800 | tf_op jit(solution)/shard_map/convert_element_type | solution.py:421
  10.7 23.0 %shard_map.158 = (f32[8,8,2880]{2,1,0:T(8,128)}, f32[4,2,20,144]{3,2,1,0:T(8,128)}) custom-call(f32[8,8,2880]{2,1,0:T(8,128)} %bitcast.21, f32[2,20,20,576]{3,2,1,0:T(8,128)} %copy_convert_fusion.refs_1_, f32[8,2880]{1,0:T(8,128)} %constant.22.clone.refs_2_, f32[8,2880]{1,0:T(8,128)} %constant.23.clone.refs_3_), custom_call_target="tpu_custom_call" | custom-call | tf_op jit(solution)/shard_map/pallas_call | solution.py:380
  33.7 24.7 %shard_map.159 = (bf16[20,8,8192]{2,1,0:T(8,128)(2,1)}, f32[20,8,8192]{2,1,0:T(8,128)}, f32[64,2880]{1,0:T(8,128)}) custom-call(f32[64,2880]{1,0:T(8,128)} %bitcast.25, bf16[20,8,8192]{2,1,0:T(8,128)(2,1)} %bitcast.20, bf16[20,8,8192]{2,1,0:T(8,128)(2,1)} %bitcast.22, bf16[20,20]{1,0:T(8,128)(2,1)} %point.1, bf16[20,20]{1,0:T(8,128)(2,1)} %bitcast.26, ...), custom_call_target="tpu_custom_call" | custom-call | tf_op jit(solution)/shard_map/pallas_call | solution.py:429
  58.4 23.3 %shard_map.160 = (f32[8,8,2880]{2,1,0:T(8,128)}, f32[4,2,20,144]{3,2,1,0:T(8,128)}, f32[4,2,20,144]{3,2,1,0:T(8,128)}) custom-call(f32[8,8,2880]{2,1,0:T(8,128)} %bitcast.23, f32[2,20,20,576]{3,2,1,0:T(8,128)} %copy_convert_fusion.refs_1_, f32[8,2880]{1,0:T(8,128)} %constant.22.clone.refs_2_, f32[8,2880]{1,0:T(8,128)} %constant.23.clone.refs_3_, ...), custom_call_target="tpu_custom_call" | custom-call | tf_op jit(solution)/shard_map/pallas_call | solution.py:380
  81.7 12.7 %shard_map.161 = (bf16[20,8,8192]{2,1,0:T(8,128)(2,1)}, f32[20,20,2,144]{3,2,1,0:T(2,128)}) custom-call(f32[64,2880]{1,0:T(8,128)} %bitcast.24, f32[20,8,8192]{2,1,0:T(8,128)} %get-tuple-element.18.local, f32[4,2,20,144]{3,2,1,0:T(8,128)} %get-tuple-element.19.spec_all, f32[4,2,20,144]{3,2,1,0:T(8,128)} %get-tuple-element.20.up_all, ...), custom_call_target="tpu_custom_call" | custom-call | tf_op jit(solution)/shard_map/pallas_call | solution.py:441
Async XLA Ops:
  0.6 8.5 %copy-start = (bf16[2,20,20,576]{3,0,2,1:T(2,128)(2,1)S(1)}, bf16[2,20,20,576]{3,0,2,1:T(2,128)(2,1)}, u32[]{:S(2)}) copy-start(bf16[2,20,20,576]{3,0,2,1:T(2,128)(2,1)} %param.16) | copy-start | bytes 2764804
where the time goes:
time: 94.5 us; the launch traced here: 94.3 us
  Pallas kernels  90.6 us (96%)
  other arithmetic  1.6 us (2%)
  local copies, waits for them, and re-layouts  1.47 us (2%)
    pallas_call x2, Pallas kernels, exchange(): pl.pallas_call(functools.partial(exchange_kernel, n, ns, backward, scale_...  46.3 us
    pallas_call x1, Pallas kernels, shards(): call(middle_kernel, (grid_bf, grid_f, part), [w_buf, g_buf, g_buf, z_buf,...  24.7 us
    pallas_call x1, Pallas kernels, shards(): call(last_kernel, (grid_bf, grad_shape), [w_buf, g_buf, g_buf])  12.7 us
    pallas_call x1, Pallas kernels, shards(): partial = call(first_kernel, part, [w_buf, z_buf, z_buf])(field, fwd, depth)  7 us

commit v1 on v0

v1 whole, which is shorter than its diff:
```python
import functools
import math

import jax
import jax.numpy as jnp
import numpy as np
from jax import lax
from jax.experimental import pallas as pl
from jax.experimental.pallas import tpu as pltpu
from jax.sharding import PartitionSpec as P

NX, NY, NZ, NT = 64, 64, 32, 4
MX, MY, MZ, MT = 12, 12, 8, 4
VOLUME = NX * NY * NZ * NT
PLANE = NZ * NT
XY = MX * MY
BF16, F32 = jnp.bfloat16, jnp.float32
VMEM_LIMIT = 60 * 1024 * 1024
GROUP = 4
MESH = pl.DeviceIdType.MESH


def signed(modes):
    index = np.arange(modes)
    return np.where(index < modes // 2, index, index - modes)


def split_np(table):
    high = table.astype(np.float32).astype(BF16)
    low = (table - high.astype(np.float64)).astype(np.float32).astype(BF16)
    return high, low


def tables(rows, space):
    fy, fx = signed(MY), signed(MX)
    y = np.arange(NY)
    x = np.arange(space * rows).reshape(space, rows)
    phi = 2 * np.pi * (
        (fy.reshape(1, MY, 1, 1, 1) * y.reshape(1, 1, 1, NY, 1) % NY) / NY
        + (fx.reshape(1, 1, MX, 1, 1) * x.reshape(space, 1, 1, 1, rows) % NX) / NX
    ).reshape(space, XY, NY * rows)
    plane = np.concatenate([np.cos(phi), np.sin(phi)], 1)
    hi, lo = split_np(plane)
    forward = np.concatenate([hi, lo], 1)
    turned = lambda t: np.transpose(t, (0, 2, 1))
    inverse = np.concatenate([turned(hi), turned(lo), turned(hi)], 2)
    fz, ft = signed(MZ), signed(MT)
    z, t = np.arange(NZ), np.arange(NT)
    psi = 2 * np.pi * (
        fz.reshape(MZ, 1, 1, 1) * z.reshape(1, 1, NZ, 1) / NZ
        + ft.reshape(1, MT, 1, 1) * t.reshape(1, 1, 1, NT) / NT
    ).reshape(space, MZ * MT // space, PLANE)
    cos, sin = np.cos(psi), np.sin(psi)
    depth = np.stack(
        [np.concatenate([cos, -sin], -1), np.concatenate([-sin, -cos], -1)], 1
    ).reshape(space, 2 * MZ * MT // space, 2 * PLANE)
    dhi, dlo = split_np(depth)
    flat = lambda t: t.reshape(2 * MZ * MT, 2 * PLANE)
    by_core = lambda t: flat(np.concatenate([t[0::2], t[1::2]], 0))
    depth_forward = np.concatenate([by_core(dhi), by_core(dlo)], 0)
    depth_inverse = np.concatenate([flat(dhi), flat(dhi), flat(dlo)], 0)
    return forward, inverse, depth_forward, depth_inverse


def split(value):
    high = value.astype(BF16)
    return high, (value - high.astype(F32)).astype(BF16)


def dot(a, b, contract=(1, 0)):
    dims = (((contract[0],), (contract[1],)), ((), ()))
    return lax.dot_general(a, b, dims, preferred_element_type=F32)


def forward_pair(block, fwd, zhi, zlo, p, exact):
    half = fwd.shape[0] // 2
    if exact:
        res = dot(fwd[...], block)
        res = res[:half] + res[half:]
    else:
        high, low = split(block)
        res = dot(fwd[...], high)
        res = res[:half] + res[half:] + dot(fwd[:half], low)
    for k in range(2):
        part = res[:, k * PLANE : (k + 1) * PLANE]
        high, low = split(jnp.concatenate([part[:XY], part[XY:]], -1))
        zhi[2 * p + k] = high
        zlo[2 * p + k] = low


def forward_depth(depth, zhi, zlo):
    rows = depth.shape[0] // 2
    high = zhi[...].reshape(-1, 2 * PLANE)
    low = zlo[...].reshape(-1, 2 * PLANE)
    first = dot(depth[...], high, (1, 1))
    return first[:rows] + first[rows:] + dot(depth[:rows], low, (1, 1))


def inverse_depth(modes, depth, grid):
    high, low = split(modes)
    stacked = jnp.concatenate([high, low, high], 0)
    lines = dot(stacked, depth[...], (0, 0)).reshape(GROUP, XY, 2 * PLANE)
    high, low = split(lines)
    for at, value in ((0, high), (2 * XY, high), (4 * XY, low)):
        grid[:, at : at + XY] = value[:, :, :PLANE]
        grid[:, at + XY : at + 2 * XY] = value[:, :, PLANE:]


def inverse_pair(inv, grid, p):
    return dot(inv[...], jnp.concatenate([grid[2 * p], grid[2 * p + 1]], -1))


def main_kernel(
    n, ns,
    fields_h, cot_h, weight_h, fwd_h, inv_h, depth_f, depth_i, point, bias_row, copies, copies_t, same,
    act_h, local_h, modes_h, spec_h, up_h,
    fields, cot, weight, fwd, inv, work, local, act, zhi, zlo, grid, pre, mix, mix_back, bias, pair_rows, w_re, w_im,
    part, near, joined, recv, modes, stage, lined, mixed, spec, got,
    load_sem, table_sem, act_sem, out_sem,
    near_send, near_recv, sum_send, sum_recv, all_send, all_recv, relay_send, relay_recv, side_send, side_recv,
):
    channels, cells, _ = fields.shape
    chunks = channels // GROUP
    rows = cells // NY
    flat = channels * rows
    chips = n // 2
    own_rows = stage.shape[1]
    owned = own_rows // 2
    per = ns // owned
    count = owned * XY // ns
    me = lax.axis_index("space")
    mine = lax.axis_index("sample")
    core = lax.rem(me, 2)
    chip = (me - core) // 2
    sibling = me + 1 - 2 * core

    barrier = pltpu.get_barrier_semaphore()
    for k in range(1, n):
        pl.semaphore_signal(barrier, inc=1, device_id={"space": lax.rem(me + k, n)}, device_id_type=MESH)
    for k in range(1, ns):
        pl.semaphore_signal(barrier, inc=1, device_id={"sample": lax.rem(mine + k, ns)}, device_id_type=MESH)

    def group(k):
        return pl.ds(k * GROUP, GROUP)

    def load(src, dst, which, k):
        return pltpu.make_async_copy(src.at[group(k)], dst.at[group(k)], load_sem.at[which, k])

    fwd_load = pltpu.make_async_copy(fwd_h.at[me], fwd, table_sem.at[0])
    inv_load = pltpu.make_async_copy(inv_h.at[me], inv, table_sem.at[1])
    weight_load = pltpu.make_async_copy(weight_h, weight, table_sem.at[2])
    fwd_load.start()
    for k in range(chunks):
        load(fields_h, fields, 0, k).start()
    weight_load.start()
    inv_load.start()
    for k in range(chunks):
        load(cot_h, cot, 1, k).start()

    def remote(src, dst, send, got_sem, axis, target):
        return pltpu.make_async_remote_copy(
            src_ref=src, dst_ref=dst, send_sem=send, recv_sem=got_sem,
            device_id={axis: target}, device_id_type=MESH,
        )

    def to_sibling(e, k):
        return remote(part.at[k, 1 - core], near.at[e, k], near_send.at[e, k], near_recv.at[e, k], "space", sibling)

    def to_owner(e, k, j):
        goal = lax.rem(chip + j, chips)
        return remote(
            joined.at[e, k, goal], recv.at[e, k, j - 1], sum_send.at[e, k, j], sum_recv.at[e, k, j], "space", 2 * goal + core
        )

    def to_all(e, k, j):
        target = lax.rem(me + 2 * j, n) if j else sibling
        return remote(modes.at[e, k, me], modes.at[e, k, me], all_send.at[e, k, j], all_recv.at[e, k, j], "space", target)

    def to_relay(e, k, j):
        block = modes.at[e, k, lax.rem(me + n - 2 * j, n)]
        return remote(block, block, relay_send.at[e, k, j], relay_recv.at[e, k, j], "space", sibling)

    def join(e, k):
        to_sibling(e, k).wait()
        total = part[k, core] + near[e, k]
        for j in range(chips):
            joined[e, k, j] = total[j * own_rows : (j + 1) * own_rows]
        for j in range(1, chips):
            to_owner(e, k, j).start()

    def put_part(k, value):
        half = value.shape[0] // 2
        part[k, 0] = value[:half]
        part[k, 1] = value[half:]

    def spread(matrix, side):
        half = dot(copies[...], matrix, (1, side)).astype(BF16)
        return dot(half, copies_t[...]).astype(BF16) * same[...]

    fwd_load.wait()
    pl.semaphore_wait(barrier, n - 1 + ns - 1)

    def first(k, carry):
        load(fields_h, fields, 0, k).wait()
        for p in range(GROUP // 2):
            c = k * GROUP + 2 * p
            forward_pair(jnp.concatenate([fields[c], fields[c + 1]], -1), fwd, zhi, zlo, p, True)
        put_part(k, forward_depth(depth_f, zhi, zlo))
        to_sibling(0, k).start()

        @pl.when(k > 0)
        def _():
            join(0, k - 1)

        return carry

    lax.fori_loop(0, chunks, first, 0)

    mix[...] = spread(point[...], 1)
    mix_back[...] = spread(point[...], 0)
    column = jnp.sum(copies[...].astype(F32) * bias_row[...], -1, keepdims=True)
    bias[...] = jnp.broadcast_to(column, (flat, PLANE))
    join(0, chunks - 1)

    weight_load.wait()

    def widen(c, carry):
        pair_rows[...] = weight[c].astype(F32)
        w_re[c] = pair_rows[:, 0, :]
        w_im[c] = pair_rows[:, 1, :]
        return carry

    lax.fori_loop(0, channels, widen, 0)

    def pointwise(i, carry):
        at = pl.multiple_of(i * 2 * rows, 2 * rows)
        block = fields[:, pl.ds(at, 2 * rows), :].astype(F32)
        block = jnp.concatenate([block[:, :rows], block[:, rows:]], -1).reshape(flat, 2 * PLANE)
        value = dot(mix[...], block.astype(BF16))
        for k in range(2):
            out = value[:, k * PLANE : (k + 1) * PLANE] + bias[...]
            work[:, pl.ds(pl.multiple_of(at + k * rows, rows), rows), :] = out.reshape(channels, rows, PLANE)
        return carry

    half_lines = NY // 4
    lax.fori_loop(0, half_lines, pointwise, 0, unroll=2)

    def gather_total(e, scale):
        for k in range(chunks):
            for j in range(1, chips):
                to_owner(e, k, j).wait()
            total = joined[e, k, chip]
            for j in range(1, chips):
                total = total + recv[e, k, j - 1]
            total = total * scale
            for g in range(GROUP):
                stage[g] = total[:, g * XY : (g + 1) * XY]
            for j in range(own_rows):
                r, q = j // owned, j % owned
                block = stage[:, j, :]
                lined[r, k * GROUP : (k + 1) * GROUP, q * XY : (q + 1) * XY] = block
                for p in range(per):
                    spec[e, q * per + p, r, k * GROUP : (k + 1) * GROUP] = block[:, p * count : (p + 1) * count]

    def side(e, j):
        goal = lax.rem(mine + j, ns)
        return remote(spec.at[e, goal], got.at[e, j], side_send.at[e, j], side_recv.at[e, j], "sample", goal)

    def scatter_mixed(e):
        for k in range(chunks):
            for j in range(own_rows):
                r, q = j // owned, j % owned
                stage[:, j, :] = mixed[r, k * GROUP : (k + 1) * GROUP, q * XY : (q + 1) * XY]
            modes[e, k, me] = jnp.concatenate([stage[g] for g in range(GROUP)], -1)
            for j in range(chips):
                to_all(e, k, j).start()

    gather_total(0, 1.0)

    def add(c, carry):
        w_r, w_i = w_re[c], w_im[c]
        s_r, s_i = lined[0, pl.ds(c, 1), :], lined[1, pl.ds(c, 1), :]
        return carry[0] + (w_r * s_r - w_i * s_i), carry[1] + (w_r * s_i + w_i * s_r)

    zero = jnp.zeros((channels, owned * XY), F32)
    real, imag = lax.fori_loop(0, channels, add, (zero, zero))
    mixed[0] = real * (1.0 / VOLUME)
    mixed[1] = imag * (1.0 / VOLUME)
    scatter_mixed(0)
    for j in range(1, ns):
        side(0, j).start()
    inv_load.wait()
    lax.fori_loop(half_lines, 2 * half_lines, pointwise, 0, unroll=2)

    def relay(e, k):
        for j in range(1, chips):
            to_all(e, k, j).wait()
            to_relay(e, k, j).start()

    def arrived(e, k):
        to_all(e, k, 0).wait()
        for j in range(1, chips):
            to_relay(e, k, j).wait()

    relay(0, 0)

    def act_store(k):
        return pltpu.make_async_copy(act.at[group(k)], act_h.at[group(k)], act_sem.at[k])

    def middle(k, carry):
        @pl.when(k + 1 < chunks)
        def _():
            relay(0, k + 1)

        arrived(0, k)
        inverse_depth(modes[0, k].reshape(n * own_rows, GROUP * XY), depth_i, grid)
        load(cot_h, cot, 1, k).wait()
        for p in range(GROUP // 2):
            pre[...] = inverse_pair(inv, grid, p)
            for h in range(2):
                c = k * GROUP + 2 * p + h
                value = pre[:, h * PLANE : (h + 1) * PLANE] + work[c]
                phi = 0.5 * (1.0 + lax.erf(value * (1.0 / math.sqrt(2.0))))
                slope = phi + value * jnp.exp(-0.5 * value * value) * (1.0 / math.sqrt(2.0 * math.pi))
                act[c] = (value * phi).astype(BF16)
                work[c] = cot[c].astype(F32) * slope
            c = k * GROUP + 2 * p
            forward_pair(jnp.concatenate([work[c], work[c + 1]], -1), fwd, zhi, zlo, p, False)
        act_store(k).start()

        put_part(k, forward_depth(depth_f, zhi, zlo))
        to_sibling(1, k).start()

        @pl.when(k > 0)
        def _():
            join(1, k - 1)

        return carry

    lax.fori_loop(0, chunks, middle, 0)

    def back(i, carry):
        at = pl.multiple_of(i * 2 * rows, 2 * rows)
        block = work[:, pl.ds(at, 2 * rows), :]
        block = jnp.concatenate([block[:, :rows], block[:, rows:]], -1).reshape(flat, 2 * PLANE)
        high, low = split(block)
        value = dot(mix_back[...], high) + dot(mix_back[...], low)
        for k in range(2):
            out = value[:, k * PLANE : (k + 1) * PLANE].reshape(channels, rows, PLANE)
            local[:, pl.ds(pl.multiple_of(at + k * rows, rows), rows), :] = out
        return carry

    lax.fori_loop(0, half_lines // 2, back, 0, unroll=2)
    join(1, chunks - 1)
    lax.fori_loop(half_lines // 2, 2 * half_lines, back, 0, unroll=2)
    local_store = pltpu.make_async_copy(local, local_h, out_sem.at[0])
    local_store.start()

    gather_total(1, 1.0 / VOLUME)
    for j in range(1, ns):
        side(1, j).start()

    def reduce(c, carry):
        w_r, w_i = w_re[c], w_im[c]
        u_r, u_i = lined[0], lined[1]
        mixed[0, pl.ds(c, 1), :] = jnp.sum(w_r * u_r + w_i * u_i, 0, keepdims=True)
        mixed[1, pl.ds(c, 1), :] = jnp.sum(w_r * u_i - w_i * u_r, 0, keepdims=True)
        return carry

    lax.fori_loop(0, channels, reduce, 0)
    scatter_mixed(1)

    for e in range(2):
        for j in range(1, ns):
            side(e, j).wait()
        got[e, 0] = spec[e, mine]
    spec_store = pltpu.make_async_copy(got.at[0], spec_h, out_sem.at[1])
    up_store = pltpu.make_async_copy(got.at[1], up_h, out_sem.at[2])
    spec_store.start()
    up_store.start()
    for k in range(chunks):
        relay(1, k)
    for k in range(chunks):
        arrived(1, k)
    modes_store = pltpu.make_async_copy(modes.at[1], modes_h, out_sem.at[3])
    modes_store.start()
    for k in range(chunks):
        act_store(k).wait()
    local_store.wait()
    spec_store.wait()
    up_store.wait()
    modes_store.wait()


def last_kernel(
    modes_h, local_h, spec_h, up_h, act_in, inv_h, depth_i,
    act_h, out_h, grad,
    modes, local, spec, up, act, inv, out, grid, load_sem, local_sem, act_sem, store_sem, pass_sem,
):
    channels = out.shape[0]
    chunks = channels // GROUP
    me = lax.axis_index("space")
    n = modes.shape[1]

    def group(k):
        return pl.ds(k * GROUP, GROUP)

    def local_load(k):
        return pltpu.make_async_copy(local_h.at[group(k)], local.at[group(k)], local_sem.at[k])

    def act_load(k):
        return pltpu.make_async_copy(act_in.at[group(k)], act.at[group(k)], act_sem.at[k])

    def act_store(k):
        return pltpu.make_async_copy(act.at[group(k)], act_h.at[group(k)], pass_sem.at[k])

    def out_store(k):
        return pltpu.make_async_copy(out.at[group(k)], out_h.at[group(k)], store_sem.at[k])

    first = [
        pltpu.make_async_copy(modes_h, modes, load_sem.at[0]),
        pltpu.make_async_copy(inv_h.at[me], inv, load_sem.at[1]),
        pltpu.make_async_copy(spec_h, spec, load_sem.at[2]),
        pltpu.make_async_copy(up_h, up, load_sem.at[3]),
    ]
    for copy in first:
        copy.start()
    for k in range(chunks):
        local_load(k).start()
        act_load(k).start()
    for copy in first:
        copy.wait()

    samples, _, _, count = spec.shape

    def chunk(k, carry):
        inverse_depth(modes[k].reshape(-1, GROUP * XY), depth_i, grid)
        local_load(k).wait()
        for p in range(GROUP // 2):
            res = inverse_pair(inv, grid, p)
            for h in range(2):
                c = k * GROUP + 2 * p + h
                out[c] = (res[:, h * PLANE : (h + 1) * PLANE] + local[c]).astype(BF16)
        out_store(k).start()
        act_load(k).wait()
        act_store(k).start()
        return carry

    lax.fori_loop(0, chunks, chunk, 0)

    def term(c, carry):
        real = jnp.zeros((channels, count), F32)
        imag = jnp.zeros((channels, count), F32)
        for s in range(samples):
            a_r, a_i = spec[s, 0, pl.ds(c, 1), :], spec[s, 1, pl.ds(c, 1), :]
            b_r, b_i = up[s, 0], up[s, 1]
            real = real + (a_r * b_r + a_i * b_i)
            imag = imag + (a_r * b_i - a_i * b_r)
        grad[c, :, 0, :] = real
        grad[c, :, 1, :] = imag
        return carry

    lax.fori_loop(0, channels, term, 0)
    for k in range(chunks):
        out_store(k).wait()
        act_store(k).wait()


def shards(fields, cotangent, spectral_weight, point_weight, point_bias):
    _, rows, channels, columns = fields.shape
    n = lax.axis_size("space")
    ns = lax.axis_size("sample")
    forward, inverse, depth_f, depth_i = [jnp.asarray(t) for t in tables(rows, n)]
    cells = NY * rows
    chunks = channels // GROUP
    chips = n // 2
    owned = MT * MZ // n
    own_rows = 2 * owned
    width = GROUP * XY
    flat = channels * rows
    count = owned * XY // ns
    copies = np.repeat(np.eye(channels), rows, 0).astype(BF16)
    same = np.tile(np.eye(rows), (channels, channels)).astype(BF16)

    def by_channel(value):
        value = value[0].reshape(rows, channels, NY, PLANE)
        return jnp.transpose(value, (1, 2, 0, 3)).reshape(channels, cells, PLANE)

    def by_row(value):
        value = jnp.transpose(value.reshape(channels, NY, rows, PLANE), (2, 0, 1, 3))
        return value.reshape(1, rows, channels, columns)

    weight = jnp.transpose(spectral_weight, (1, 2, 0, 3))
    vmem, dma = pltpu.VMEM, pltpu.SemaphoreType.DMA
    any_spec, vmem_spec = pl.BlockSpec(memory_space=pl.ANY), pl.BlockSpec(memory_space=vmem)
    shape = jax.ShapeDtypeStruct
    kept = (ns, 2, channels, count)
    grid_bf = shape((channels, cells, PLANE), BF16)
    grid_f = shape((channels, cells, PLANE), F32)
    modes_shape = (chunks, n, own_rows, width)

    act, local, modes, spec, up = pl.pallas_call(
        functools.partial(main_kernel, n, ns),
        out_shape=[grid_bf, grid_f, shape(modes_shape, F32), shape(kept, F32), shape(kept, F32)],
        in_specs=[any_spec] * 5 + [vmem_spec] * 7,
        out_specs=[any_spec] * 5,
        scratch_shapes=[
            vmem((channels, cells, PLANE), BF16),
            vmem((channels, cells, PLANE), BF16),
            vmem(weight.shape, BF16),
            vmem(forward.shape[1:], BF16),
            vmem(inverse.shape[1:], BF16),
            vmem((channels, cells, PLANE), F32),
            vmem((channels, cells, PLANE), F32),
            vmem((channels, cells, PLANE), BF16),
            vmem((GROUP, XY, 2 * PLANE), BF16),
            vmem((GROUP, XY, 2 * PLANE), BF16),
            vmem((GROUP, 6 * XY, PLANE), BF16),
            vmem((cells, 2 * PLANE), F32),
            vmem((flat, flat), BF16),
            vmem((flat, flat), BF16),
            vmem((flat, PLANE), F32),
            vmem((channels, 2, owned * XY), F32),
            vmem((channels, channels, owned * XY), F32),
            vmem((channels, channels, owned * XY), F32),
            vmem((chunks, 2, chips * own_rows, width), F32),
            vmem((2, chunks, chips * own_rows, width), F32),
            vmem((2, chunks, chips, own_rows, width), F32),
            vmem((2, chunks, chips - 1, own_rows, width), F32),
            vmem((2,) + modes_shape, F32),
            vmem((GROUP, own_rows, XY), F32),
            vmem((2, channels, owned * XY), F32),
            vmem((2, channels, owned * XY), F32),
            vmem((2,) + kept, F32),
            vmem((2,) + kept, F32),
            dma((2, chunks)), dma((3,)), dma((chunks,)), dma((4,)),
            dma((2, chunks)), dma((2, chunks)),
            dma((2, chunks, chips)), dma((2, chunks, chips)),
            dma((2, chunks, chips)), dma((2, chunks, chips)),
            dma((2, chunks, chips)), dma((2, chunks, chips)),
            dma((2, ns)), dma((2, ns)),
        ],
        compiler_params=pltpu.CompilerParams(
            vmem_limit_bytes=VMEM_LIMIT, collective_id=0, has_side_effects=True
        ),
    )(
        by_channel(fields), by_channel(cotangent), weight, forward, inverse, depth_f, depth_i,
        point_weight, point_bias[None], copies, copies.T, same,
    )

    act_out, grad_in, grad = pl.pallas_call(
        last_kernel,
        out_shape=[grid_bf, grid_bf, shape((channels, channels, 2, count), F32)],
        in_specs=[any_spec] * 6 + [vmem_spec],
        out_specs=[any_spec, any_spec, vmem_spec],
        scratch_shapes=[
            vmem(modes_shape, F32),
            vmem((channels, cells, PLANE), F32),
            vmem(kept, F32),
            vmem(kept, F32),
            vmem((channels, cells, PLANE), BF16),
            vmem(inverse.shape[1:], BF16),
            vmem((channels, cells, PLANE), BF16),
            vmem((GROUP, 6 * XY, PLANE), BF16),
            dma((4,)), dma((chunks,)), dma((chunks,)), dma((chunks,)), dma((chunks,)),
        ],
        compiler_params=pltpu.CompilerParams(vmem_limit_bytes=VMEM_LIMIT),
    )(modes, local, spec, up, act, inverse, depth_i)
    return by_row(act_out), by_row(grad_in), jnp.transpose(grad, (2, 0, 1, 3))


def solution(mesh):
    return jax.shard_map(
        shards,
        mesh=mesh,
        in_specs=(
            P("sample", "space", None, None),
            P("sample", "space", None, None),
            P(None, None, None, "space"),
            P(),
            P(),
        ),
        out_specs=(
            P("sample", "space", None, None),
            P("sample", "space", None, None),
            P(None, None, None, ("space", "sample")),
        ),
        check_vma=False,
    )
```

time: 94.5 us -> 64.1 us (0.68)
  Pallas kernels: 90.6 us -> 63.2 us
  other arithmetic: 1.6 us -> 0 us
  local copies, waits for them, and re-layouts: 1.47 us -> 0 us
    pallas_call x5 -> x2, Pallas kernels: 90.6 us -> 63.2 us  [the longest x1 51.9 us: shards(): pl.pallas_call(functools.partial(main_kernel, n, ns), out_shape=[grid_bf,...]
    convert_element_type x1 -> x0, other arithmetic: 1.6 us -> none  [shards(): weights = spectral_weight.astype(F32)]
    unnamed x3 -> x0, local copies, waits for them, and re-layouts: 1.47 us -> none
where the time goes in v1:
time: 64.1 us; the launch traced here: 63.9 us
  Pallas kernels  63.2 us (99%)
    pallas_call x1, Pallas kernels, shards(): pl.pallas_call(functools.partial(main_kernel, n, ns), out_shape=[grid_bf,...  51.9 us
    pallas_call x1, Pallas kernels, shards(): pl.pallas_call(last_kernel, out_shape=[grid_bf, grid_bf, shape((channels,...  11.3 us

profile of v1, /device:TPU:0, one launch (start us, length us, event | category | flops | bytes accessed | tf_op | source)
XLA Modules:
  0.0 63.9 jit_solution(9871546599381688339)
XLA Ops:
  0.6 51.9 %shard_map.139 = (bf16[20,512,128]{2,1,0:T(8,128)(2,1)}, f32[20,512,128]{2,1,0:T(8,128)}, f32[5,8,8,576]{3,2,1,0:T(8,128)}, f32[4,2,20,144]{3,2,1,0:T(8,128)}, f32[4,2,20,144]{3,2,1,0:T(8,128)}) custom-call(bf16[20,512,128]{2,1,0:T(8,128)(2,1)} %bitcast.23, bf16[20,512,128]{2,1,0:T(8,128)(2,1)} %bitcast.24, bf16[20,20,2,576]{3,2,1,0:T(2,128)(2,1)} %bitcast.25, ...), custom_call_target="tpu_custom_call" | custom-call | tf_op jit(solution)/shard_map/pallas_call | solution.py:502
  52.6 11.3 %shard_map.140 = (bf16[20,512,128]{2,1,0:T(8,128)(2,1)}, bf16[20,512,128]{2,1,0:T(8,128)(2,1)}, f32[20,20,2,144]{3,2,1,0:T(2,128)}) custom-call(f32[5,8,8,576]{3,2,1,0:T(8,128)} %get-tuple-element.11.modes_h, f32[20,512,128]{2,1,0:T(8,128)} %get-tuple-element.12.local_h, f32[4,2,20,144]{3,2,1,0:T(8,128)} %get-tuple-element.13.spec_h, ...), custom_call_target="tpu_custom_call" | custom-call | tf_op jit(solution)/shard_map/pallas_call | solution.py:551

commit v2 on v1

--- a/solution.py
+++ b/solution.py
@@ -15,7 +15,7 @@
 PLANE = NZ * NT
 XY = MX * MY
 BF16, F32 = jnp.bfloat16, jnp.float32
-VMEM_LIMIT = 60 * 1024 * 1024
+VMEM_LIMIT = 44 * 1024 * 1024
 GROUP = 4
 MESH = pl.DeviceIdType.MESH
 
@@ -113,10 +113,10 @@
 def main_kernel(
     n, ns,
     fields_h, cot_h, weight_h, fwd_h, inv_h, depth_f, depth_i, point, bias_row, copies, copies_t, same,
-    act_h, local_h, modes_h, spec_h, up_h,
-    fields, cot, weight, fwd, inv, work, local, act, zhi, zlo, grid, pre, mix, mix_back, bias, pair_rows, w_re, w_im,
+    act, out, grad,
+    fields, cot, weight, fwd, inv, work, local, zhi, zlo, grid, pre, mix, mix_back, bias, pair_rows, w_re, w_im,
     part, near, joined, recv, modes, stage, lined, mixed, spec, got,
-    load_sem, table_sem, act_sem, out_sem,
+    load_sem, table_sem,
     near_send, near_recv, sum_send, sum_recv, all_send, all_recv, relay_send, relay_recv, side_send, side_recv,
 ):
     channels, cells, _ = fields.shape
@@ -304,9 +304,6 @@
 
     relay(0, 0)
 
-    def act_store(k):
-        return pltpu.make_async_copy(act.at[group(k)], act_h.at[group(k)], act_sem.at[k])
-
     def middle(k, carry):
         @pl.when(k + 1 < chunks)
         def _():
@@ -326,7 +323,6 @@
                 work[c] = cot[c].astype(F32) * slope
             c = k * GROUP + 2 * p
             forward_pair(jnp.concatenate([work[c], work[c + 1]], -1), fwd, zhi, zlo, p, False)
-        act_store(k).start()
 
         put_part(k, forward_depth(depth_f, zhi, zlo))
         to_sibling(1, k).start()
@@ -353,8 +349,6 @@
     lax.fori_loop(0, half_lines // 2, back, 0, unroll=2)
     join(1, chunks - 1)
     lax.fori_loop(half_lines // 2, 2 * half_lines, back, 0, unroll=2)
-    local_store = pltpu.make_async_copy(local, local_h, out_sem.at[0])
-    local_store.start()
 
     gather_total(1, 1.0 / VOLUME)
     for j in range(1, ns):
@@ -369,101 +363,42 @@
 
     lax.fori_loop(0, channels, reduce, 0)
     scatter_mixed(1)
+    relay(1, 0)
 
     for e in range(2):
         for j in range(1, ns):
             side(e, j).wait()
         got[e, 0] = spec[e, mine]
-    spec_store = pltpu.make_async_copy(got.at[0], spec_h, out_sem.at[1])
-    up_store = pltpu.make_async_copy(got.at[1], up_h, out_sem.at[2])
-    spec_store.start()
-    up_store.start()
-    for k in range(chunks):
-        relay(1, k)
-    for k in range(chunks):
+
+    def term(c, carry):
+        real = jnp.zeros((channels, count), F32)
+        imag = jnp.zeros((channels, count), F32)
+        for s in range(ns):
+            a_r, a_i = got[0, s, 0, pl.ds(c, 1), :], got[0, s, 1, pl.ds(c, 1), :]
+            b_r, b_i = got[1, s, 0], got[1, s, 1]
+            real = real + (a_r * b_r + a_i * b_i)
+            imag = imag + (a_r * b_i - a_i * b_r)
+        grad[c, :, 0, :] = real
+        grad[c, :, 1, :] = imag
+        return carry
+
+    lax.fori_loop(0, channels, term, 0)
+
+    def last(k, carry):
+        @pl.when(k + 1 < chunks)
+        def _():
+            relay(1, k + 1)
+
         arrived(1, k)
-    modes_store = pltpu.make_async_copy(modes.at[1], modes_h, out_sem.at[3])
-    modes_store.start()
-    for k in range(chunks):
-        act_store(k).wait()
-    local_store.wait()
-    spec_store.wait()
-    up_store.wait()
-    modes_store.wait()
-
-
-def last_kernel(
-    modes_h, local_h, spec_h, up_h, act_in, inv_h, depth_i,
-    act_h, out_h, grad,
-    modes, local, spec, up, act, inv, out, grid, load_sem, local_sem, act_sem, store_sem, pass_sem,
-):
-    channels = out.shape[0]
-    chunks = channels // GROUP
-    me = lax.axis_index("space")
-    n = modes.shape[1]
-
-    def group(k):
-        return pl.ds(k * GROUP, GROUP)
-
-    def local_load(k):
-        return pltpu.make_async_copy(local_h.at[group(k)], local.at[group(k)], local_sem.at[k])
-
-    def act_load(k):
-        return pltpu.make_async_copy(act_in.at[group(k)], act.at[group(k)], act_sem.at[k])
-
-    def act_store(k):
-        return pltpu.make_async_copy(act.at[group(k)], act_h.at[group(k)], pass_sem.at[k])
-
-    def out_store(k):
-        return pltpu.make_async_copy(out.at[group(k)], out_h.at[group(k)], store_sem.at[k])
-
-    first = [
-        pltpu.make_async_copy(modes_h, modes, load_sem.at[0]),
-        pltpu.make_async_copy(inv_h.at[me], inv, load_sem.at[1]),
-        pltpu.make_async_copy(spec_h, spec, load_sem.at[2]),
-        pltpu.make_async_copy(up_h, up, load_sem.at[3]),
-    ]
-    for copy in first:
-        copy.start()
-    for k in range(chunks):
-        local_load(k).start()
-        act_load(k).start()
-    for copy in first:
-        copy.wait()
-
-    samples, _, _, count = spec.shape
-
-    def chunk(k, carry):
-        inverse_depth(modes[k].reshape(-1, GROUP * XY), depth_i, grid)
-        local_load(k).wait()
+        inverse_depth(modes[1, k].reshape(n * own_rows, GROUP * XY), depth_i, grid)
         for p in range(GROUP // 2):
             res = inverse_pair(inv, grid, p)
             for h in range(2):
                 c = k * GROUP + 2 * p + h
                 out[c] = (res[:, h * PLANE : (h + 1) * PLANE] + local[c]).astype(BF16)
-        out_store(k).start()
-        act_load(k).wait()
-        act_store(k).start()
-        return carry
-
-    lax.fori_loop(0, chunks, chunk, 0)
-
-    def term(c, carry):
-        real = jnp.zeros((channels, count), F32)
-        imag = jnp.zeros((channels, count), F32)
-        for s in range(samples):
-            a_r, a_i = spec[s, 0, pl.ds(c, 1), :], spec[s, 1, pl.ds(c, 1), :]
-            b_r, b_i = up[s, 0], up[s, 1]
-            real = real + (a_r * b_r + a_i * b_i)
-            imag = imag + (a_r * b_i - a_i * b_r)
-        grad[c, :, 0, :] = real
-        grad[c, :, 1, :] = imag
-        return carry
-
-    lax.fori_loop(0, channels, term, 0)
-    for k in range(chunks):
-        out_store(k).wait()
-        act_store(k).wait()
+        return carry
+
+    lax.fori_loop(0, chunks, last, 0)
 
 
 def shards(fields, cotangent, spectral_weight, point_weight, point_bias):
@@ -492,18 +427,19 @@
 
     weight = jnp.transpose(spectral_weight, (1, 2, 0, 3))
     vmem, dma = pltpu.VMEM, pltpu.SemaphoreType.DMA
-    any_spec, vmem_spec = pl.BlockSpec(memory_space=pl.ANY), pl.BlockSpec(memory_space=vmem)
-    shape = jax.ShapeDtypeStruct
+    any_spec, vmem_spec = pl.BlockSpec(memory_space=pltpu.HBM), pl.BlockSpec(memory_space=vmem)
     kept = (ns, 2, channels, count)
-    grid_bf = shape((channels, cells, PLANE), BF16)
-    grid_f = shape((channels, cells, PLANE), F32)
     modes_shape = (chunks, n, own_rows, width)
 
-    act, local, modes, spec, up = pl.pallas_call(
+    act, grad_in, grad = pl.pallas_call(
         functools.partial(main_kernel, n, ns),
-        out_shape=[grid_bf, grid_f, shape(modes_shape, F32), shape(kept, F32), shape(kept, F32)],
+        out_shape=[
+            vmem((channels, cells, PLANE), BF16),
+            vmem((channels, cells, PLANE), BF16),
+            vmem((channels, channels, 2, count), F32),
+        ],
         in_specs=[any_spec] * 5 + [vmem_spec] * 7,
-        out_specs=[any_spec] * 5,
+        out_specs=[vmem_spec] * 3,
         scratch_shapes=[
             vmem((channels, cells, PLANE), BF16),
             vmem((channels, cells, PLANE), BF16),
@@ -512,7 +448,6 @@
             vmem(inverse.shape[1:], BF16),
             vmem((channels, cells, PLANE), F32),
             vmem((channels, cells, PLANE), F32),
-            vmem((channels, cells, PLANE), BF16),
             vmem((GROUP, XY, 2 * PLANE), BF16),
             vmem((GROUP, XY, 2 * PLANE), BF16),
             vmem((GROUP, 6 * XY, PLANE), BF16),
@@ -533,7 +468,7 @@
             vmem((2, channels, owned * XY), F32),
             vmem((2,) + kept, F32),
             vmem((2,) + kept, F32),
-            dma((2, chunks)), dma((3,)), dma((chunks,)), dma((4,)),
+            dma((2, chunks)), dma((3,)),
             dma((2, chunks)), dma((2, chunks)),
             dma((2, chunks, chips)), dma((2, chunks, chips)),
             dma((2, chunks, chips)), dma((2, chunks, chips)),
@@ -548,25 +483,7 @@
         point_weight, point_bias[None], copies, copies.T, same,
     )
 
-    act_out, grad_in, grad = pl.pallas_call(
-        last_kernel,
-        out_shape=[grid_bf, grid_bf, shape((channels, channels, 2, count), F32)],
-        in_specs=[any_spec] * 6 + [vmem_spec],
-        out_specs=[any_spec, any_spec, vmem_spec],
-        scratch_shapes=[
-            vmem(modes_shape, F32),
-            vmem((channels, cells, PLANE), F32),
-            vmem(kept, F32),
-            vmem(kept, F32),
-            vmem((channels, cells, PLANE), BF16),
-            vmem(inverse.shape[1:], BF16),
-            vmem((channels, cells, PLANE), BF16),
-            vmem((GROUP, 6 * XY, PLANE), BF16),
-            dma((4,)), dma((chunks,)), dma((chunks,)), dma((chunks,)), dma((chunks,)),
-        ],
-        compiler_params=pltpu.CompilerParams(vmem_limit_bytes=VMEM_LIMIT),
-    )(modes, local, spec, up, act, inverse, depth_i)
-    return by_row(act_out), by_row(grad_in), jnp.transpose(grad, (2, 0, 1, 3))
+    return by_row(act), by_row(grad_in), jnp.transpose(grad, (2, 0, 1, 3))
 
 
 def solution(mesh):

time: 64.1 us -> 65.6 us (1.023)
  local copies, waits for them, and re-layouts: 0 us -> 12.3 us
  Pallas kernels: 63.2 us -> 52.2 us
    unnamed x0 -> x21, local copies, waits for them, and re-layouts: none -> 12.3 us
    pallas_call x2 -> x1, Pallas kernels: 63.2 us -> 52.2 us  [shards(): pl.pallas_call(functools.partial(main_kernel, n, ns), out_shape=[vmem((ch...]
where the time goes in v2:
time: 65.6 us; the launch traced here: 65.2 us
  Pallas kernels  52.2 us (80%)
  local copies, waits for them, and re-layouts  12.3 us (19%)
  between operations  0.66 us (1%)
    pallas_call x1, Pallas kernels, shards(): pl.pallas_call(functools.partial(main_kernel, n, ns), out_shape=[vmem((ch...  52.2 us
    unnamed x21, local copies, waits for them, and re-layouts  12.3 us

profile of v2, /device:TPU:0, one launch (start us, length us, event | category | flops | bytes accessed | tf_op | source)
XLA Modules:
  0.0 65.2 jit_solution(15802964416275578851)
XLA Ops:
  0.6 0.0 copy-start
  0.6 1.7 %copy-done = bf16[1,8,20,8192]{3,1,2,0:T(8,128)(2,1)S(1)} copy-done((bf16[1,8,20,8192]{3,1,2,0:T(8,128)(2,1)S(1)}, bf16[1,8,20,8192]{3,1,2,0:T(8,128)(2,1)}, u32[]{:S(2)}) %copy-start) | copy-done | bytes 2621464
  2.4 0.0 copy-start.1
  2.4 1.2 %copy-done.1 = bf16[2,20,20,576]{3,0,2,1:T(2,128)(2,1)S(1)} copy-done((bf16[2,20,20,576]{3,0,2,1:T(2,128)(2,1)S(1)}, bf16[2,20,20,576]{3,0,2,1:T(2,128)(2,1)}, u32[]{:S(2)}) %copy-start.1) | copy-done | bytes 921624
  3.6 0.0 copy-start.2
  3.6 0.9 %copy-done.2 = bf16[192,256]{1,0:T(8,128)(2,1)S(1)} copy-done((bf16[192,256]{1,0:T(8,128)(2,1)S(1)}, bf16[192,256]{1,0:T(8,128)(2,1)}, u32[]{:S(2)}) %copy-start.2) | copy-done | bytes 98328
  4.5 0.0 copy-start.3
  4.5 0.9 %copy-done.3 = bf16[160,160]{1,0:T(8,128)(2,1)S(1)} copy-done((bf16[160,160]{1,0:T(8,128)(2,1)S(1)}, bf16[160,160]{1,0:T(8,128)(2,1)}, u32[]{:S(2)}) %copy-start.3) | copy-done | bytes 51224
  5.4 0.0 copy-start.4
  5.4 0.8 %copy-done.4 = bf16[128,256]{1,0:T(8,128)(2,1)S(1)} copy-done((bf16[128,256]{1,0:T(8,128)(2,1)S(1)}, bf16[128,256]{1,0:T(8,128)(2,1)}, u32[]{:S(2)}) %copy-start.4) | copy-done | bytes 65560
  6.2 0.0 copy-start.5
  6.2 0.8 %copy-done.5 = bf16[160,20]{1,0:T(8,128)(2,1)S(1)} copy-done((bf16[160,20]{1,0:T(8,128)(2,1)S(1)}, bf16[160,20]{1,0:T(8,128)(2,1)}, u32[]{:S(2)}) %copy-start.5) | copy-done | bytes 6424
  7.0 0.0 copy-start.6
  7.0 0.7 %copy-done.6 = bf16[20,160]{1,0:T(8,128)(2,1)S(1)} copy-done((bf16[20,160]{1,0:T(8,128)(2,1)S(1)}, bf16[20,160]{1,0:T(8,128)(2,1)}, u32[]{:S(2)}) %copy-start.6) | copy-done | bytes 6424
  7.7 0.0 copy-start.7
  7.7 0.7 %copy-done.7 = bf16[20,20]{1,0:T(8,128)(2,1)S(1)} copy-done((bf16[20,20]{1,0:T(8,128)(2,1)S(1)}, bf16[20,20]{1,0:T(8,128)(2,1)}, u32[]{:S(2)}) %copy-start.7) | copy-done | bytes 824
  8.4 0.0 copy-start.8
  8.4 0.7 %copy-done.8 = f32[20]{0:T(128)S(1)} copy-done((f32[20]{0:T(128)S(1)}, f32[20]{0:T(128)}, u32[]{:S(2)}) %copy-start.8) | copy-done | bytes 104
  9.0 52.2 %shard_map.139 = (bf16[20,512,128]{2,1,0:T(8,128)(2,1)S(1)}, bf16[20,512,128]{2,1,0:T(8,128)(2,1)S(1)}, f32[20,20,2,144]{3,2,1,0:T(2,128)S(1)}) custom-call(bf16[20,512,128]{2,1,0:T(8,128)(2,1)S(1)} %bitcast.26, bf16[20,512,128]{2,1,0:T(8,128)(2,1)} %bitcast.29, bf16[20,20,2,576]{3,2,1,0:T(2,128)(2,1)S(1)} %bitcast.27, ...), custom_call_target="tpu_custom_call" | custom-call | tf_op jit(solution)/shard_map/pallas_call | solution.py:434
  61.3 1.5 %copy.18 = bf16[1,8,20,8192]{3,1,2,0:T(8,128)(2,1)} copy(bf16[1,8,20,8192]{3,1,2,0:T(8,128)(2,1)S(1)} %bitcast.24) | data formatting | bytes 5242880
  62.8 1.5 %copy.19 = bf16[1,8,20,8192]{3,1,2,0:T(8,128)(2,1)} copy(bf16[1,8,20,8192]{3,1,2,0:T(8,128)(2,1)S(1)} %bitcast.23) | data formatting | bytes 5242880
  64.3 0.9 %copy.20 = f32[2,20,20,144]{3,0,2,1:T(2,128)} copy(f32[2,20,20,144]{3,0,2,1:T(2,128)S(1)} %bitcast.25) | data formatting | bytes 921600
Async XLA Ops:
  0.6 1.7 %copy-start = (bf16[1,8,20,8192]{3,1,2,0:T(8,128)(2,1)S(1)}, bf16[1,8,20,8192]{3,1,2,0:T(8,128)(2,1)}, u32[]{:S(2)}) copy-start(bf16[1,8,20,8192]{3,1,2,0:T(8,128)(2,1)} %param.12) | copy-start | bytes 7864324
  2.4 1.2 %copy-start.1 = (bf16[2,20,20,576]{3,0,2,1:T(2,128)(2,1)S(1)}, bf16[2,20,20,576]{3,0,2,1:T(2,128)(2,1)}, u32[]{:S(2)}) copy-start(bf16[2,20,20,576]{3,0,2,1:T(2,128)(2,1)} %param.14) | copy-start | bytes 2764804
  3.6 0.9 %copy-start.2 = (bf16[192,256]{1,0:T(8,128)(2,1)S(1)}, bf16[192,256]{1,0:T(8,128)(2,1)}, u32[]{:S(2)}) copy-start(bf16[192,256]{1,0:T(8,128)(2,1)} %constant.17.clone.depth_i) | copy-start | bytes 294916
  4.5 0.9 %copy-start.3 = (bf16[160,160]{1,0:T(8,128)(2,1)S(1)}, bf16[160,160]{1,0:T(8,128)(2,1)}, u32[]{:S(2)}) copy-start(bf16[160,160]{1,0:T(8,128)(2,1)} %constant.20.clone.same) | copy-start | bytes 153604
  5.4 0.8 %copy-start.4 = (bf16[128,256]{1,0:T(8,128)(2,1)S(1)}, bf16[128,256]{1,0:T(8,128)(2,1)}, u32[]{:S(2)}) copy-start(bf16[128,256]{1,0:T(8,128)(2,1)} %constant.16.clone.depth_f) | copy-start | bytes 196612
  6.2 0.8 %copy-start.5 = (bf16[160,20]{1,0:T(8,128)(2,1)S(1)}, bf16[160,20]{1,0:T(8,128)(2,1)}, u32[]{:S(2)}) copy-start(bf16[160,20]{1,0:T(8,128)(2,1)} %constant.18.clone.copies) | copy-start | bytes 19204
  7.0 0.7 %copy-start.6 = (bf16[20,160]{1,0:T(8,128)(2,1)S(1)}, bf16[20,160]{1,0:T(8,128)(2,1)}, u32[]{:S(2)}) copy-start(bf16[20,160]{1,0:T(8,128)(2,1)} %constant.19.clone.copies_t) | copy-start | bytes 19204
  7.7 0.7 %copy-start.7 = (bf16[20,20]{1,0:T(8,128)(2,1)S(1)}, bf16[20,20]{1,0:T(8,128)(2,1)}, u32[]{:S(2)}) copy-start(bf16[20,20]{1,0:T(8,128)(2,1)} %point.1) | copy-start | bytes 2404
  8.4 0.7 %copy-start.8 = (f32[20]{0:T(128)S(1)}, f32[20]{0:T(128)}, u32[]{:S(2)}) copy-start(f32[20]{0:T(128)} %param.16) | copy-start | bytes 244

commit v3 on v2

--- a/solution.py
+++ b/solution.py
@@ -15,7 +15,7 @@
 PLANE = NZ * NT
 XY = MX * MY
 BF16, F32 = jnp.bfloat16, jnp.float32
-VMEM_LIMIT = 44 * 1024 * 1024
+VMEM_LIMIT = 60_970_000
 GROUP = 4
 MESH = pl.DeviceIdType.MESH
 

time: 65.6 us -> 58.3 us (0.89)
  local copies, waits for them, and re-layouts: 12.3 us -> 3.88 us
  Pallas kernels: 52.2 us -> 53.7 us
    unnamed x21 -> x3, local copies, waits for them, and re-layouts: 12.3 us -> 3.88 us
    pallas_call x1, Pallas kernels: 52.2 us -> 53.7 us  [shards(): pl.pallas_call(functools.partial(main_kernel, n, ns), out_shape=[vmem((ch...]
where the time goes in v3:
time: 58.3 us; the launch traced here: 58.2 us
  Pallas kernels  53.7 us (92%)
  local copies, waits for them, and re-layouts  3.88 us (7%)
  between operations  0.64 us (1%)
    pallas_call x1, Pallas kernels, shards(): pl.pallas_call(functools.partial(main_kernel, n, ns), out_shape=[vmem((ch...  53.7 us
    unnamed x3, local copies, waits for them, and re-layouts  3.88 us

profile of v3, /device:TPU:0, one launch (start us, length us, event | category | flops | bytes accessed | tf_op | source)
XLA Modules:
  0.0 58.2 jit_solution(10682546868685951537)
XLA Ops:
  0.6 53.7 %shard_map.139 = (bf16[20,512,128]{2,1,0:T(8,128)(2,1)S(1)}, bf16[20,512,128]{2,1,0:T(8,128)(2,1)S(1)}, f32[20,20,2,144]{3,2,1,0:T(2,128)S(1)}) custom-call(bf16[20,512,128]{2,1,0:T(8,128)(2,1)} %bitcast.26, bf16[20,512,128]{2,1,0:T(8,128)(2,1)} %bitcast.27, bf16[20,20,2,576]{3,2,1,0:T(2,128)(2,1)} %bitcast.28, bf16[8,576,512]{2,1,0:T(8,128)(2,1)} %constant.14.clone.fwd_h, ...), custom_call_target="tpu_custom_call" | custom-call | tf_op jit(solution)/shard_map/pallas_call | solution.py:434
  54.3 1.5 %copy.18 = bf16[1,8,20,8192]{3,1,2,0:T(8,128)(2,1)} copy(bf16[1,8,20,8192]{3,1,2,0:T(8,128)(2,1)S(1)} %bitcast.24) | data formatting | bytes 5242880
  55.8 1.5 %copy.19 = bf16[1,8,20,8192]{3,1,2,0:T(8,128)(2,1)} copy(bf16[1,8,20,8192]{3,1,2,0:T(8,128)(2,1)S(1)} %bitcast.23) | data formatting | bytes 5242880
  57.3 0.9 %copy.20 = f32[2,20,20,144]{3,0,2,1:T(2,128)} copy(f32[2,20,20,144]{3,0,2,1:T(2,128)S(1)} %bitcast.25) | data formatting | bytes 921600

commit v4 on v3

--- a/solution.py
+++ b/solution.py
@@ -112,13 +112,14 @@
 
 def main_kernel(
     n, ns,
-    fields_h, cot_h, weight_h, fwd_h, inv_h, depth_f, depth_i, point, bias_row, copies, copies_t, same,
-    act, out, grad,
-    fields, cot, weight, fwd, inv, work, local, zhi, zlo, grid, pre, mix, mix_back, bias, pair_rows, w_re, w_im,
-    part, near, joined, recv, modes, stage, lined, mixed, spec, got,
-    load_sem, table_sem,
-    near_send, near_recv, sum_send, sum_recv, all_send, all_recv, relay_send, relay_recv, side_send, side_recv,
+    fields_h, cot_h, weight_h, fwd_h, inv_h, *refs,
 ):
+    smalls_h, (act, out, grad), smalls, refs = refs[:7], refs[7:10], refs[10:17], refs[17:]
+    depth_f, depth_i, point, bias_row, copies, copies_t, same = smalls
+    (fields, cot, weight, fwd, inv, work, local, zhi, zlo, grid, pre, mix, mix_back, bias, pair_rows, w_re, w_im,
+     part, near, joined, recv, modes, stage, lined, mixed, spec, got,
+     load_sem, table_sem, small_sem,
+     near_send, near_recv, sum_send, sum_recv, all_send, all_recv, relay_send, relay_recv, side_send, side_recv) = refs
     channels, cells, _ = fields.shape
     chunks = channels // GROUP
     rows = cells // NY
@@ -149,8 +150,14 @@
     fwd_load = pltpu.make_async_copy(fwd_h.at[me], fwd, table_sem.at[0])
     inv_load = pltpu.make_async_copy(inv_h.at[me], inv, table_sem.at[1])
     weight_load = pltpu.make_async_copy(weight_h, weight, table_sem.at[2])
+    small_loads = [
+        pltpu.make_async_copy(src, dst, small_sem.at[i]) for i, (src, dst) in enumerate(zip(smalls_h, smalls))
+    ]
     fwd_load.start()
-    for k in range(chunks):
+    load(fields_h, fields, 0, 0).start()
+    for copy in small_loads:
+        copy.start()
+    for k in range(1, chunks):
         load(fields_h, fields, 0, k).start()
     weight_load.start()
     inv_load.start()
@@ -198,23 +205,27 @@
         return dot(half, copies_t[...]).astype(BF16) * same[...]
 
     fwd_load.wait()
-    pl.semaphore_wait(barrier, n - 1 + ns - 1)
-
-    def first(k, carry):
+
+    def transform(k):
         load(fields_h, fields, 0, k).wait()
         for p in range(GROUP // 2):
             c = k * GROUP + 2 * p
             forward_pair(jnp.concatenate([fields[c], fields[c + 1]], -1), fwd, zhi, zlo, p, True)
+
+    def first(k, carry):
+        transform(k)
         put_part(k, forward_depth(depth_f, zhi, zlo))
         to_sibling(0, k).start()
-
-        @pl.when(k > 0)
-        def _():
-            join(0, k - 1)
-
-        return carry
-
-    lax.fori_loop(0, chunks, first, 0)
+        join(0, k - 1)
+        return carry
+
+    transform(0)
+    for copy in small_loads:
+        copy.wait()
+    put_part(0, forward_depth(depth_f, zhi, zlo))
+    pl.semaphore_wait(barrier, n - 1 + ns - 1)
+    to_sibling(0, 0).start()
+    lax.fori_loop(1, chunks, first, 0)
 
     mix[...] = spread(point[...], 1)
     mix_back[...] = spread(point[...], 0)
@@ -245,7 +256,7 @@
     half_lines = NY // 4
     lax.fori_loop(0, half_lines, pointwise, 0, unroll=2)
 
-    def gather_total(e, scale):
+    def gather_total(e, scale, use=None):
         for k in range(chunks):
             for j in range(1, chips):
                 to_owner(e, k, j).wait()
@@ -261,6 +272,8 @@
                 lined[r, k * GROUP : (k + 1) * GROUP, q * XY : (q + 1) * XY] = block
                 for p in range(per):
                     spec[e, q * per + p, r, k * GROUP : (k + 1) * GROUP] = block[:, p * count : (p + 1) * count]
+            if use is not None:
+                use(k)
 
     def side(e, j):
         goal = lax.rem(mine + j, ns)
@@ -275,17 +288,18 @@
             for j in range(chips):
                 to_all(e, k, j).start()
 
-    gather_total(0, 1.0)
-
-    def add(c, carry):
-        w_r, w_i = w_re[c], w_im[c]
-        s_r, s_i = lined[0, pl.ds(c, 1), :], lined[1, pl.ds(c, 1), :]
-        return carry[0] + (w_r * s_r - w_i * s_i), carry[1] + (w_r * s_i + w_i * s_r)
-
-    zero = jnp.zeros((channels, owned * XY), F32)
-    real, imag = lax.fori_loop(0, channels, add, (zero, zero))
-    mixed[0] = real * (1.0 / VOLUME)
-    mixed[1] = imag * (1.0 / VOLUME)
+    def add(k):
+        real, imag = (mixed[0], mixed[1]) if k else (0.0, 0.0)
+        for c in range(k * GROUP, (k + 1) * GROUP):
+            w_r, w_i = w_re[c], w_im[c]
+            s_r, s_i = lined[0, c : c + 1, :], lined[1, c : c + 1, :]
+            real = real + (w_r * s_r - w_i * s_i)
+            imag = imag + (w_r * s_i + w_i * s_r)
+        scale = 1.0 / VOLUME if k == chunks - 1 else 1.0
+        mixed[0] = real * scale
+        mixed[1] = imag * scale
+
+    gather_total(0, 1.0, add)
     scatter_mixed(0)
     for j in range(1, ns):
         side(0, j).start()
@@ -399,6 +413,15 @@
         return carry
 
     lax.fori_loop(0, chunks, last, 0)
+
+
+def store_kernel(*refs):
+    sources, goals, sem = refs[:3], refs[3:6], refs[6]
+    copies = [pltpu.make_async_copy(a, b, sem.at[i]) for i, (a, b) in enumerate(zip(sources, goals))]
+    for copy in copies:
+        copy.start()
+    for copy in copies:
+        copy.wait()
 
 
 def shards(fields, cotangent, spectral_weight, point_weight, point_bias):
@@ -431,6 +454,7 @@
     kept = (ns, 2, channels, count)
     modes_shape = (chunks, n, own_rows, width)
 
+    smalls = [depth_f, depth_i, point_weight, point_bias[None], copies, copies.T, same]
     act, grad_in, grad = pl.pallas_call(
         functools.partial(main_kernel, n, ns),
         out_shape=[
@@ -438,9 +462,9 @@
             vmem((channels, cells, PLANE), BF16),
             vmem((channels, channels, 2, count), F32),
         ],
-        in_specs=[any_spec] * 5 + [vmem_spec] * 7,
+        in_specs=[any_spec] * 12,
         out_specs=[vmem_spec] * 3,
-        scratch_shapes=[
+        scratch_shapes=[vmem(t.shape, t.dtype) for t in smalls] + [
             vmem((channels, cells, PLANE), BF16),
             vmem((channels, cells, PLANE), BF16),
             vmem(weight.shape, BF16),
@@ -468,7 +492,7 @@
             vmem((2, channels, owned * XY), F32),
             vmem((2,) + kept, F32),
             vmem((2,) + kept, F32),
-            dma((2, chunks)), dma((3,)),
+            dma((2, chunks)), dma((3,)), dma((7,)),
             dma((2, chunks)), dma((2, chunks)),
             dma((2, chunks, chips)), dma((2, chunks, chips)),
             dma((2, chunks, chips)), dma((2, chunks, chips)),
@@ -479,10 +503,17 @@
             vmem_limit_bytes=VMEM_LIMIT, collective_id=0, has_side_effects=True
         ),
     )(
-        by_channel(fields), by_channel(cotangent), weight, forward, inverse, depth_f, depth_i,
-        point_weight, point_bias[None], copies, copies.T, same,
+        by_channel(fields), by_channel(cotangent), weight, forward, inverse, *smalls
     )
 
+    act, grad_in, grad = pl.pallas_call(
+        store_kernel,
+        out_shape=[jax.ShapeDtypeStruct(v.shape, v.dtype) for v in (act, grad_in, grad)],
+        in_specs=[vmem_spec] * 3,
+        out_specs=[any_spec] * 3,
+        scratch_shapes=[dma((3,))],
+        compiler_params=pltpu.CompilerParams(vmem_limit_bytes=512 * 1024),
+    )(act, grad_in, grad)
     return by_row(act), by_row(grad_in), jnp.transpose(grad, (2, 0, 1, 3))
 
 

time: 58.3 us -> 56.3 us (0.966)
  local copies, waits for them, and re-layouts: 3.88 us -> 0 us
  Pallas kernels: 53.7 us -> 55.5 us
    unnamed x3 -> x0, local copies, waits for them, and re-layouts: 3.88 us -> none
    pallas_call x0 -> x1, Pallas kernels: none -> 2.64 us  [shards(): pl.pallas_call(store_kernel, out_shape=[jax.ShapeDtypeStruct(v.shape, v.d...]
    pallas_call x1, Pallas kernels: 53.7 us -> 52.9 us  [shards(): pl.pallas_call(functools.partial(main_kernel, n, ns), out_shape=[vmem((ch...]
where the time goes in v4:
time: 56.3 us; the launch traced here: 56.2 us
  Pallas kernels  55.5 us (99%)
  between operations  0.64 us (1%)
    pallas_call x1, Pallas kernels, shards(): pl.pallas_call(functools.partial(main_kernel, n, ns), out_shape=[vmem((ch...  52.9 us
    pallas_call x1, Pallas kernels, shards(): pl.pallas_call(store_kernel, out_shape=[jax.ShapeDtypeStruct(v.shape, v.d...  2.64 us

profile of v4, /device:TPU:0, one launch (start us, length us, event | category | flops | bytes accessed | tf_op | source)
XLA Modules:
  0.0 56.2 jit_solution(12659042435572326483)
XLA Ops:
  0.6 52.9 %shard_map.139 = (bf16[20,512,128]{2,1,0:T(8,128)(2,1)S(1)}, bf16[20,512,128]{2,1,0:T(8,128)(2,1)S(1)}, f32[20,20,2,144]{3,2,1,0:T(2,128)S(1)}) custom-call(bf16[20,512,128]{2,1,0:T(8,128)(2,1)} %bitcast.23, bf16[20,512,128]{2,1,0:T(8,128)(2,1)} %bitcast.24, bf16[20,20,2,576]{3,2,1,0:T(2,128)(2,1)} %bitcast.25, bf16[8,576,512]{2,1,0:T(8,128)(2,1)} %constant.14.clone.fwd_h, ...), custom_call_target="tpu_custom_call" | custom-call | tf_op jit(solution)/shard_map/pallas_call | solution.py:458
  53.5 2.6 %shard_map.140 = (bf16[20,512,128]{2,1,0:T(8,128)(2,1)}, bf16[20,512,128]{2,1,0:T(8,128)(2,1)}, f32[20,20,2,144]{3,2,1,0:T(2,128)}) custom-call(bf16[20,512,128]{2,1,0:T(8,128)(2,1)S(1)} %get-tuple-element.9.refs_0_, bf16[20,512,128]{2,1,0:T(8,128)(2,1)S(1)} %get-tuple-element.10.refs_1_, f32[20,20,2,144]{3,2,1,0:T(2,128)S(1)} %get-tuple-element.11.refs_2_), custom_call_target="tpu_custom_call" | custom-call | tf_op jit(solution)/shard_map/pallas_call | solution.py:509

commit v5 on v4

--- a/solution.py
+++ b/solution.py
@@ -173,18 +173,24 @@
     def to_sibling(e, k):
         return remote(part.at[k, 1 - core], near.at[e, k], near_send.at[e, k], near_recv.at[e, k], "space", sibling)
 
+    def partner(j):
+        if chips == 4:
+            pair = (chip, 3 - chip, lax.rem(chip + 2, 4), chip + 1 - 2 * lax.rem(chip, 2))[j]
+            return pair, pair
+        return lax.rem(chip + j, chips), lax.rem(chip + chips - j, chips)
+
     def to_owner(e, k, j):
-        goal = lax.rem(chip + j, chips)
+        goal = partner(j)[0]
         return remote(
             joined.at[e, k, goal], recv.at[e, k, j - 1], sum_send.at[e, k, j], sum_recv.at[e, k, j], "space", 2 * goal + core
         )
 
     def to_all(e, k, j):
-        target = lax.rem(me + 2 * j, n) if j else sibling
+        target = 2 * partner(j)[0] + core if j else sibling
         return remote(modes.at[e, k, me], modes.at[e, k, me], all_send.at[e, k, j], all_recv.at[e, k, j], "space", target)
 
     def to_relay(e, k, j):
-        block = modes.at[e, k, lax.rem(me + n - 2 * j, n)]
+        block = modes.at[e, k, 2 * partner(j)[1] + core]
         return remote(block, block, relay_send.at[e, k, j], relay_recv.at[e, k, j], "space", sibling)
 
     def join(e, k):
@@ -285,7 +291,7 @@
                 r, q = j // owned, j % owned
                 stage[:, j, :] = mixed[r, k * GROUP : (k + 1) * GROUP, q * XY : (q + 1) * XY]
             modes[e, k, me] = jnp.concatenate([stage[g] for g in range(GROUP)], -1)
-            for j in range(chips):
+            for j in list(range(1, chips)) + [0]:
                 to_all(e, k, j).start()
 
     def add(k):
@@ -362,7 +368,7 @@
 
     lax.fori_loop(0, half_lines // 2, back, 0, unroll=2)
     join(1, chunks - 1)
-    lax.fori_loop(half_lines // 2, 2 * half_lines, back, 0, unroll=2)
+    lax.fori_loop(half_lines // 2, 3 * half_lines // 2, back, 0, unroll=2)
 
     gather_total(1, 1.0 / VOLUME)
     for j in range(1, ns):
@@ -377,12 +383,8 @@
 
     lax.fori_loop(0, channels, reduce, 0)
     scatter_mixed(1)
+    lax.fori_loop(3 * half_lines // 2, 2 * half_lines, back, 0, unroll=2)
     relay(1, 0)
-
-    for e in range(2):
-        for j in range(1, ns):
-            side(e, j).wait()
-        got[e, 0] = spec[e, mine]
 
     def term(c, carry):
         real = jnp.zeros((channels, count), F32)
@@ -396,12 +398,18 @@
         grad[c, :, 1, :] = imag
         return carry
 
-    lax.fori_loop(0, channels, term, 0)
-
     def last(k, carry):
         @pl.when(k + 1 < chunks)
         def _():
             relay(1, k + 1)
+
+        @pl.when(k + 1 == chunks)
+        def _():
+            for e in range(2):
+                for j in range(1, ns):
+                    side(e, j).wait()
+                got[e, 0] = spec[e, mine]
+            lax.fori_loop(0, channels, term, 0)
 
         arrived(1, k)
         inverse_depth(modes[1, k].reshape(n * own_rows, GROUP * XY), depth_i, grid)

time: 56.3 us -> 54.1 us (0.961)
  Pallas kernels: 55.5 us -> 53.3 us
    pallas_call x1, Pallas kernels: 52.9 us -> 50.7 us  [shards(): pl.pallas_call(functools.partial(main_kernel, n, ns), out_shape=[vmem((ch...]
where the time goes in v5:
time: 54.1 us; the launch traced here: 53.9 us
  Pallas kernels  53.3 us (99%)
  between operations  0.64 us (1%)
    pallas_call x1, Pallas kernels, shards(): pl.pallas_call(functools.partial(main_kernel, n, ns), out_shape=[vmem((ch...  50.7 us
    pallas_call x1, Pallas kernels, shards(): pl.pallas_call(store_kernel, out_shape=[jax.ShapeDtypeStruct(v.shape, v.d...  2.64 us

profile of v5, /device:TPU:0, one launch (start us, length us, event | category | flops | bytes accessed | tf_op | source)
XLA Modules:
  0.0 53.9 jit_solution(3911158399020404995)
XLA Ops:
  0.6 50.7 %shard_map.139 = (bf16[20,512,128]{2,1,0:T(8,128)(2,1)S(1)}, bf16[20,512,128]{2,1,0:T(8,128)(2,1)S(1)}, f32[20,20,2,144]{3,2,1,0:T(2,128)S(1)}) custom-call(bf16[20,512,128]{2,1,0:T(8,128)(2,1)} %bitcast.23, bf16[20,512,128]{2,1,0:T(8,128)(2,1)} %bitcast.24, bf16[20,20,2,576]{3,2,1,0:T(2,128)(2,1)} %bitcast.25, bf16[8,576,512]{2,1,0:T(8,128)(2,1)} %constant.14.clone.fwd_h, ...), custom_call_target="tpu_custom_call" | custom-call | tf_op jit(solution)/shard_map/pallas_call | solution.py:466
  51.3 2.6 %shard_map.140 = (bf16[20,512,128]{2,1,0:T(8,128)(2,1)}, bf16[20,512,128]{2,1,0:T(8,128)(2,1)}, f32[20,20,2,144]{3,2,1,0:T(2,128)}) custom-call(bf16[20,512,128]{2,1,0:T(8,128)(2,1)S(1)} %get-tuple-element.9.refs_0_, bf16[20,512,128]{2,1,0:T(8,128)(2,1)S(1)} %get-tuple-element.10.refs_1_, f32[20,20,2,144]{3,2,1,0:T(2,128)S(1)} %get-tuple-element.11.refs_2_), custom_call_target="tpu_custom_call" | custom-call | tf_op jit(solution)/shard_map/pallas_call | solution.py:517

commit v6 on v5

--- a/solution.py
+++ b/solution.py
@@ -333,10 +333,11 @@
         inverse_depth(modes[0, k].reshape(n * own_rows, GROUP * XY), depth_i, grid)
         load(cot_h, cot, 1, k).wait()
         for p in range(GROUP // 2):
-            pre[...] = inverse_pair(inv, grid, p)
+            pre[p] = inverse_pair(inv, grid, p)
+        for p in range(GROUP // 2):
             for h in range(2):
                 c = k * GROUP + 2 * p + h
-                value = pre[:, h * PLANE : (h + 1) * PLANE] + work[c]
+                value = pre[p, :, h * PLANE : (h + 1) * PLANE] + work[c]
                 phi = 0.5 * (1.0 + lax.erf(value * (1.0 / math.sqrt(2.0))))
                 slope = phi + value * jnp.exp(-0.5 * value * value) * (1.0 / math.sqrt(2.0 * math.pi))
                 act[c] = (value * phi).astype(BF16)
@@ -425,7 +426,11 @@
 
 def store_kernel(*refs):
     sources, goals, sem = refs[:3], refs[3:6], refs[6]
-    copies = [pltpu.make_async_copy(a, b, sem.at[i]) for i, (a, b) in enumerate(zip(sources, goals))]
+    copies = []
+    for k in range(sem.shape[1]):
+        for i in range(3):
+            piece = pl.ds(k * GROUP, GROUP)
+            copies.append(pltpu.make_async_copy(sources[i].at[piece], goals[i].at[piece], sem.at[i, k]))
     for copy in copies:
         copy.start()
     for copy in copies:
@@ -483,7 +488,7 @@
             vmem((GROUP, XY, 2 * PLANE), BF16),
             vmem((GROUP, XY, 2 * PLANE), BF16),
             vmem((GROUP, 6 * XY, PLANE), BF16),
-            vmem((cells, 2 * PLANE), F32),
+            vmem((GROUP // 2, cells, 2 * PLANE), F32),
             vmem((flat, flat), BF16),
             vmem((flat, flat), BF16),
             vmem((flat, PLANE), F32),
@@ -519,7 +524,7 @@
         out_shape=[jax.ShapeDtypeStruct(v.shape, v.dtype) for v in (act, grad_in, grad)],
         in_specs=[vmem_spec] * 3,
         out_specs=[any_spec] * 3,
-        scratch_shapes=[dma((3,))],
+        scratch_shapes=[dma((3, chunks))],
         compiler_params=pltpu.CompilerParams(vmem_limit_bytes=512 * 1024),
     )(act, grad_in, grad)
     return by_row(act), by_row(grad_in), jnp.transpose(grad, (2, 0, 1, 3))

time: 54.1 us -> 53.2 us (0.983)
  Pallas kernels: 53.3 us -> 52.4 us
    pallas_call x1, Pallas kernels: 50.7 us -> 49.7 us  [shards(): pl.pallas_call(functools.partial(main_kernel, n, ns), out_shape=[vmem((ch...]
where the time goes in v6:
time: 53.2 us; the launch traced here: 53 us
  Pallas kernels  52.4 us (98%)
  between operations  0.64 us (1%)
    pallas_call x1, Pallas kernels, shards(): pl.pallas_call(functools.partial(main_kernel, n, ns), out_shape=[vmem((ch...  49.7 us
    pallas_call x1, Pallas kernels, shards(): pl.pallas_call(store_kernel, out_shape=[jax.ShapeDtypeStruct(v.shape, v.d...  2.7 us

profile of v6, /device:TPU:0, one launch (start us, length us, event | category | flops | bytes accessed | tf_op | source)
XLA Modules:
  0.0 53.0 jit_solution(12937096734584984276)
XLA Ops:
  0.6 49.7 %shard_map.139 = (bf16[20,512,128]{2,1,0:T(8,128)(2,1)S(1)}, bf16[20,512,128]{2,1,0:T(8,128)(2,1)S(1)}, f32[20,20,2,144]{3,2,1,0:T(2,128)S(1)}) custom-call(bf16[20,512,128]{2,1,0:T(8,128)(2,1)} %bitcast.23, bf16[20,512,128]{2,1,0:T(8,128)(2,1)} %bitcast.24, bf16[20,20,2,576]{3,2,1,0:T(2,128)(2,1)} %bitcast.25, bf16[8,576,512]{2,1,0:T(8,128)(2,1)} %constant.14.clone.fwd_h, ...), custom_call_target="tpu_custom_call" | custom-call | tf_op jit(solution)/shard_map/pallas_call | solution.py:471
  50.3 2.7 %shard_map.140 = (bf16[20,512,128]{2,1,0:T(8,128)(2,1)}, bf16[20,512,128]{2,1,0:T(8,128)(2,1)}, f32[20,20,2,144]{3,2,1,0:T(2,128)}) custom-call(bf16[20,512,128]{2,1,0:T(8,128)(2,1)S(1)} %get-tuple-element.9.refs_0_, bf16[20,512,128]{2,1,0:T(8,128)(2,1)S(1)} %get-tuple-element.10.refs_1_, f32[20,20,2,144]{3,2,1,0:T(2,128)S(1)} %get-tuple-element.11.refs_2_), custom_call_target="tpu_custom_call" | custom-call | tf_op jit(solution)/shard_map/pallas_call | solution.py:522
